TPU v7x, 512 devices: a whole 4x8x8 slice. The times are simulated.
512 devices in a mesh: seq: 128 (over y_hi, z, x), book: 4 (over y_lo, core).
Axes of the slice: x: 4, y: 8 (y_hi: 4, y_lo: 2; y = y_hi * 2 + y_lo), z: 8, core: 2. Of those that a mesh axis runs over, the one named last changes fastest.
Arguments:
- features: bfloat16 [4, 16384, 512], P('book', 'seq'), may hold values from -6 to 6
- lengths: int32 [4, 8], P('book'), may hold values from 1 to 4096, 16384 in all within a row
- owner: int32 [4, 16384, 1], P('book', 'seq'), may hold values from 0 to 127; in each aligned block of 128 rows (0 to 127, 128 to 255, ..., all dimensions but the last counted through in order) at most 2 rows name the same one
- w_enc: bfloat16 [3, 512, 256], replicated, may hold values from -0.15625 to 0.15625
- w_in: bfloat16 [256, 2048], P(None, ('seq', 'book')), may hold values from -0.375 to 0.375
- gain: float32 [2048], replicated, may hold values from 0.1 to 1.9
- cotangent: bfloat16 [4, 32768, 2048], P('book', 'seq'), may hold values from -24 to 24
Outputs:
- grad_features: bfloat16 [4, 16384, 512], P('book', 'seq')
- grad_w_enc: float32 [3, 512, 256], P(None, 'book')
- grad_w_in: float32 [256, 2048], P(None, ('seq', 'book'))
- grad_gain: float32 [2048], replicated
Inputs may be any that keep to these rules, and one draw needn't show every extreme that they name: Of the 128 frames of one device's block no more than 2 have the same owner, and in some block exactly 2 do. The 8 lengths of a stream sum to 16384; the largest is 4096.
All inputs are finite; a program needn't handle non-finite values.
Results may differ from a plain program's by a relative error of at most 0.0095.
Values may be sent and summed in bfloat16 or wider, within the bound.
A program may use at most 64 MiB of HBM per device.

v0:
```python
import jax
import jax.numpy as jnp
from jax import lax
from jax.sharding import PartitionSpec as P


def shifted(block, axis, distance):
    devices = range(lax.axis_size(axis))
    route = [(i - distance, i) for i in devices if i - distance in devices]
    return lax.ppermute(block, axis, route)


def book_mask(position, book_lengths, offset):
    starts = jnp.cumsum(book_lengths) - book_lengths
    start_of = jnp.max(jnp.where(starts[None, :] <= position[:, None], starts[None, :], 0), axis=1)
    return position - offset >= start_of


def per_device(features, lengths, owner, w_enc, w_in, gain, cotangent):
    feature_rows = features[0]
    frames, channels = feature_rows.shape
    tap_count, _, latent_width = w_enc.shape
    seq_count = lax.axis_size("seq")
    book_count = lax.axis_size("book")
    capacity = max(2, frames // seq_count + 1)
    first_frame = lax.axis_index("seq") * frames
    position = first_frame + jnp.arange(frames + tap_count - 1, dtype=jnp.int32)
    tap_masks = [book_mask(position, lengths[0], offset) for offset in range(tap_count)]
    feats_wide = feature_rows.astype(jnp.float32)
    activated = jax.nn.elu(feats_wide).astype(jnp.bfloat16)
    left_edge = shifted(activated[frames - (tap_count - 1) :], "seq", 1)
    padded = jnp.concatenate([left_edge, activated], axis=0)
    tap_inputs = []
    for offset in range(tap_count):
        begin = tap_count - 1 - offset
        window = padded[begin : begin + frames]
        tap_inputs.append(
            jnp.where(tap_masks[offset][:frames, None], window, jnp.zeros_like(window))
        )
    stacked = jnp.concatenate(tap_inputs, axis=1)
    latent = jnp.dot(
        stacked,
        w_enc.reshape(tap_count * channels, latent_width),
        preferred_element_type=jnp.float32,
    ).astype(jnp.bfloat16)
    owner_rank = owner[0, :, 0]
    one_hot = (owner_rank[:, None] == jnp.arange(seq_count, dtype=jnp.int32)[None, :]).astype(
        jnp.int32
    )
    slot_rank = jnp.sum((jnp.cumsum(one_hot, axis=0) - one_hot) * one_hot, axis=1)
    slot_index = owner_rank * capacity + slot_rank
    placement = (
        slot_index[:, None] == jnp.arange(seq_count * capacity, dtype=jnp.int32)[None, :]
    ).astype(jnp.bfloat16)
    outgoing = lax.dot_general(
        placement, latent, (((0,), (0,)), ((), ())), preferred_element_type=jnp.float32
    ).astype(jnp.bfloat16)
    arrived = lax.all_to_all(
        outgoing.reshape(seq_count, capacity, latent_width),
        "seq",
        split_axis=0,
        concat_axis=0,
        tiled=True,
    )
    arrived = arrived.reshape(seq_count * capacity, latent_width)
    w_full = lax.all_gather(w_in, ("seq", "book"), axis=1, tiled=True)
    grad_out = cotangent[0].astype(jnp.float32)
    hidden = jnp.dot(arrived, w_full, preferred_element_type=jnp.float32)
    inv_rms = lax.rsqrt(jnp.mean(hidden * hidden, axis=1, keepdims=True) + 1e-05)
    normed = hidden * inv_rms
    gain_term = grad_out * gain[None, :]
    hidden_grad = (
        inv_rms * (gain_term - normed * jnp.mean(gain_term * normed, axis=1, keepdims=True))
    ).astype(jnp.bfloat16)
    latent_back = lax.dot_general(
        hidden_grad, w_full, (((1,), (1,)), ((), ())), preferred_element_type=jnp.float32
    ).astype(jnp.bfloat16)
    w_part = lax.dot_general(
        arrived, hidden_grad, (((0,), (0,)), ((), ())), preferred_element_type=jnp.float32
    )
    gain_part = jnp.sum(grad_out * normed, axis=0)
    returned = lax.all_to_all(
        latent_back.reshape(seq_count, capacity, latent_width),
        "seq",
        split_axis=0,
        concat_axis=0,
        tiled=True,
    )
    returned = returned.reshape(seq_count * capacity, latent_width)
    latent_grad = jnp.dot(placement, returned, preferred_element_type=jnp.float32).astype(
        jnp.bfloat16
    )
    right_edge = shifted(latent_grad[: tap_count - 1], "seq", -1)
    extended = jnp.concatenate([latent_grad, right_edge], axis=0)
    tap_grads = []
    for offset in range(tap_count):
        window = extended[offset : offset + frames]
        tap_grads.append(
            jnp.where(
                tap_masks[offset][offset : offset + frames, None], window, jnp.zeros_like(window)
            )
        )
    kernel_back = jnp.transpose(w_enc, (0, 2, 1)).reshape(tap_count * latent_width, channels)
    activ_grad = jnp.dot(
        jnp.concatenate(tap_grads, axis=1), kernel_back, preferred_element_type=jnp.float32
    )
    slope = jnp.where(feats_wide > 0, 1.0, jnp.exp(feats_wide))
    feature_grad = (slope * activ_grad).astype(jnp.bfloat16)
    kernel_part = lax.dot_general(
        stacked, latent_grad, (((0,), (0,)), ((), ())), preferred_element_type=jnp.float32
    )
    kernel_part = kernel_part.reshape(tap_count, channels, latent_width)
    kernel_total, gain_total = lax.psum((kernel_part, gain_part), ("seq", "book"))
    share_width = channels // book_count
    kernel_mine = lax.dynamic_slice_in_dim(
        kernel_total, lax.axis_index("book") * share_width, share_width, 1
    )
    w_grad = lax.psum_scatter(w_part, ("seq", "book"), scatter_dimension=1, tiled=True)
    return (feature_grad[None], kernel_mine, w_grad, gain_total)


def solution(mesh):
    placed = (
        P("book", "seq", None),
        P("book", None),
        P("book", "seq", None),
        P(),
        P(None, ("seq", "book")),
        P(),
        P("book", "seq", None),
    )
    return jax.shard_map(
        per_device,
        mesh=mesh,
        in_specs=placed,
        out_specs=(P("book", "seq", None), P(None, "book", None), P(None, ("seq", "book")), P()),
        check_vma=False,
    )
```

profile of v0, /device:TPU:1, one launch (start us, length us, event | category | flops | bytes accessed | tf_op | source)
XLA Modules:
  0.0 1101.2 jit_solution(2386968315070701871)
XLA Ops:
  7.2 1.0 fusion.10
  8.2 3.9 collective-permute-start
  12.2 0.7 fusion.25
  13.0 0.8 reduce-window_clone.1
  13.8 0.2 reduce_window_sum.20
  14.0 0.7 subtract_bitcast_fusion
  14.7 0.8 select_reduce_fusion
  15.6 1.0 broadcast_select_fusion
  16.7 0.7 multiply_add_fusion
  17.5 1.6 convolution_convert_fusion.1
  19.2 32.3 %all_to_all.10 = bf16[128,2,256]{2,1,0:T(2,128)(2,1)S(1)} all-to-all(bf16[128,2,256]{2,1,0:T(2,128)(2,1)S(1)} %reshape.71), channel_id=1, replica_groups=mesh['seq'=128,'book'=4] {'seq'}, dimensions={0} | all-to-all | bytes 262144 | tf_op jit(solution)/shard_map/all_to_all | solution.py:58
  51.5 730.3 %all-gather.3.cloned.1.call-done = bf16[512,4,256]{2,1,0:T(4,128)(2,1)} async-done(((bf16[1,4,256]{2,1,0:T(4,128)(2,1)}), bf16[512,4,256]{2,1,0:T(4,128)(2,1)}) %all-gather.3.cloned.1.call-update) | async-done | bytes 1048592 | tf_op jit(solution)/shard_map/all_gather | solution.py:66
  781.8 1.3 reshape.80
  783.2 0.6 multiply_reduce_fusion
  783.7 0.6 copy-done
  784.4 0.8 fusion.5
  785.2 0.5 fusion.4
  785.7 0.4 convolution_convert_fusion
  786.2 0.7 reshape.73
  786.9 11.6 %all-to-all-start.1 = ((bf16[128,2,256]{2,1,0:T(2,128)(2,1)}), bf16[128,2,256]{2,1,0:T(2,128)(2,1)S(1)}, u32[]{:S(2)}, u32[]{:S(2)}) async-start(bf16[128,2,256]{2,1,0:T(2,128)(2,1)} %reshape.73), calls=%async_computation.1 | async-start | bytes 262144 | tf_op jit(solution)/shard_map/all_to_all | solution.py:82
  798.5 1.9 fusion.33
  800.3 11.2 %all-to-all-done.1 = bf16[128,2,256]{2,1,0:T(2,128)(2,1)S(1)} async-done(((bf16[128,2,256]{2,1,0:T(2,128)(2,1)}), bf16[128,2,256]{2,1,0:T(2,128)(2,1)S(1)}, u32[]{:S(2)}, u32[]{:S(2)}) %all-to-all-start.1) | async-done | bytes 131104 | tf_op jit(solution)/shard_map/all_to_all | solution.py:82
  811.6 0.2 convolution_convert_fusion.3
  811.8 1.6 fusion.16
  813.4 1.1 copy-done.1
  814.5 0.3 copy.13
  814.8 1.3 collective-permute-start.1
  816.1 98.3 %psum.15 = f32[2048]{0:T(1024)} all-reduce(f32[2048]{0:T(1024)S(1)} %get-tuple-element.4), channel_id=1, replica_groups=mesh['seq'=128,'book'=4] {'seq','book'}, use_global_device_ids=true, to_apply=%region_9.10 | all-reduce | flops 2048 | bytes 16384 | tf_op jit(solution)/shard_map/psum | solution.py:113
  914.5 0.9 fusion.7
  915.5 175.8 %all-reduce.4.cloned.1.call-done = (f32[3,512,256]{2,1,0:T(8,128)}, f32[256,2048]{0,1:T(8,128)}) async-done(((f32[3,512,256]{2,1,0:T(8,128)}, f32[256,2048]{0,1:T(8,128)}), (f32[3,512,256]{2,1,0:T(8,128)}, f32[256,2048]{0,1:T(8,128)})) %all-reduce.4.cloned.1.call-update) | async-done | bytes 3670032 | tf_op jit(solution)/shard_map/psum | solution.py:113
  1091.3 1.8 constant_dynamic-slice_fusion.1
  1093.1 1.3 constant_dynamic-slice_fusion
  (25 shorter events, 0.7 us)
Async XLA Ops:
  7.2 774.6 %all-gather.3.cloned.1.call-start = ((), (), s32[]{:S(2)}) async-start(), calls=%async_computation.2 | async-start | bytes 1050624 | tf_op jit(solution)/shard_map/all_gather | solution.py:66
  8.2 9.1 collective-permute-start
  783.2 1.2 copy-start
  783.2 1.2 copy-start.3
  786.9 24.7 %all-to-all-start.1 = ((bf16[128,2,256]{2,1,0:T(2,128)(2,1)}), bf16[128,2,256]{2,1,0:T(2,128)(2,1)S(1)}, u32[]{:S(2)}, u32[]{:S(2)}) async-start(bf16[128,2,256]{2,1,0:T(2,128)(2,1)} %reshape.73), calls=%async_computation.1 | async-start | bytes 262144 | tf_op jit(solution)/shard_map/all_to_all | solution.py:82
  798.4 292.9 %all-reduce.4.cloned.1.call-start = ((), (), s32[]{:S(2)}) async-start(), calls=%async_computation.3 | async-start | bytes 7340032 | tf_op jit(solution)/shard_map/psum | solution.py:113
  813.4 1.1 copy-start.1
  813.4 101.1 %copy-start.2 = (bf16[1,128,512]{2,1,0:T(8,128)(2,1)S(1)}, bf16[1,128,512]{2,1,0:T(8,128)(2,1)}, u32[]{:S(2)}) copy-start(bf16[1,128,512]{2,1,0:T(8,128)(2,1)} %param.7) | copy-start | bytes 393220
  814.8 99.6 %collective-permute-start.1 = (bf16[2,256]{1,0:T(2,128)(2,1)S(1)}, bf16[2,256]{1,0:T(2,128)(2,1)S(1)}, u32[]{:S(2)}, u32[]{:S(2)}) collective-permute-start(bf16[2,256]{1,0:T(2,128)(2,1)S(1)} %slice.48), channel_id=1, source_target_pairs={{4,0},{8,4},{12,8},{16,12},{20,16},{24,20},{28,24},{32,28},{36,32}... | collective-permute-start | bytes 3080 | tf_op jit(solution)/shard_map/ppermute | solution.py:10
Sparse Core Ops, SparseCore 0:
  12.3 769.4 all-gather.2
  813.5 277.6 all-reduce.3
where the time goes:
time: 1100 us
  waiting for transfers between devices  917 us (83%)
  blocking collectives  131 us (12%)
  starting transfers between devices  16.9 us (2%)
  between operations  14.2 us (1%)
    all_gather x1, waiting for transfers between devices, per_device(): w_full = lax.all_gather(w_in, ('seq', 'book'), axis=1, tiled=True)  730 us
    psum x1, waiting for transfers between devices, per_device(): lax.psum((kernel_part, gain_part), ('seq', 'book'))  176 us
    psum x1, blocking collectives, per_device(): lax.psum((kernel_part, gain_part), ('seq', 'book'))  98.3 us
    all_to_all x1, blocking collectives, per_device(): lax.all_to_all(outgoing.reshape(seq_count, capacity, latent_width), 'seq'...  32.3 us
  transfers between devices with their start and end apart: 5, of which 3 were waited for; matrix products, arithmetic and copies ran while one was open for 1% of the time, Pallas kernels for 0%

commit v1 on v0

v1 whole, which is shorter than its diff:
```python
import functools

import jax
import jax.numpy as jnp
from jax import lax
from jax.experimental import pallas as pl
from jax.experimental.pallas import tpu as pltpu
from jax.sharding import PartitionSpec as P

NX, NZ, NH, NL, NC = 4, 8, 4, 2, 2
NY = NH * NL
NSEQ = NX * NZ * NH
FR, CH, LAT, DM, CAP = 128, 512, 256, 2048, 2
ROWS = NSEQ * CAP
EPS = 1e-05
BF, F32, I32 = jnp.bfloat16, jnp.float32, jnp.int32
NT = (((1,), (1,)), ((), ()))
NN = (((1,), (0,)), ((), ()))
TN = (((0,), (0,)), ((), ()))
NSEM = 144


def dot(a, b, dims):
    return lax.dot_general(a, b, dims, preferred_element_type=F32)


def kernel(
    feat_ref, lens_ref, owner_ref, wpad_ref, gain_ref, wenc_any, cot_any,
    gf_ref, ge_ref, gw_ref, gg_ref,
    cot, wenc, ext, edge_s, edge_r, win, bkr, wf,
    a_out, r1, r2, pbuf, r3, arr2, hid, hg,
    lbuf, b1, c2, b2, b3, lext, edge2_s, edge2_r,
    as0, ar0, aown, s0, axr, s1, azr, s2, ayr, s3, acr,
    gs, gcr, gxr, gzr, gyr, gacc,
    efull, es0, er0, exs, exr, ezs, ezr, eys, eyr, gz, gx,
    send_sem, recv_sem, local_sem,
):
    seq, book = lax.axis_index("seq"), lax.axis_index("book")
    h, z, x = seq // (NZ * NX), (seq // NX) % NZ, seq % NX
    l, c = book // NC, book % NC
    y = h * NL + l
    other = 1 - c

    def dev(h=h, z=z, x=x, l=l, c=c):
        return ((h * NZ + z) * NX + x, l * NC + c)

    def dev_x(p):
        return dev(x=p)

    def dev_z(p):
        return dev(z=p)

    def dev_h(p):
        return dev(h=p)

    def dev_y(p):
        return dev(h=p // NL, l=p % NL)

    def dev_c(p):
        return dev(c=p)

    def dev_b(p):
        return dev(l=p // NC, c=p % NC)

    right = (lax.rem(seq + 1, NSEQ), book)
    left = (lax.rem(seq + NSEQ - 1, NSEQ), book)

    count = [0]
    started = []

    def push(src, dst, to):
        k = count[0]
        count[0] += 1
        copy = pltpu.make_async_remote_copy(
            src_ref=src, dst_ref=dst, send_sem=send_sem.at[k], recv_sem=recv_sem.at[k],
            device_id=to, device_id_type=pl.DeviceIdType.MESH,
        )
        copy.start()
        started.append(copy)
        return copy

    def spread(n, me, src, dst, to):
        order = sorted(range(1, n), key=lambda d: -min(d, n - d))
        copies = []
        for d in order:
            p = lax.rem(me + d, n)
            copies.append(push(src(p), dst, to(p)))
        return copies

    def landed(copies):
        for copy in copies:
            copy.wait_recv()

    barrier = pltpu.get_barrier_semaphore()
    partners = [right, left]
    for n, me, to in ((NX, x, dev_x), (NZ, z, dev_z), (NY, y, dev_y)):
        for d in range(1, n):
            partners.append(to(lax.rem(me + d, n)))
    partners.append(dev_c(other))
    partners.append(dev(l=1 - l, c=other))
    for to in partners:
        pl.semaphore_signal(barrier, inc=1, device_id=to, device_id_type=pl.DeviceIdType.MESH)

    load_w = pltpu.make_async_copy(wenc_any, wenc, local_sem.at[0])
    load_c = pltpu.make_async_copy(cot_any, cot, local_sem.at[1])
    load_w.start()
    load_c.start()

    feats = feat_ref[...].astype(F32)
    low = jnp.minimum(feats, 0.0)
    act = jnp.where(feats > 0, feats, (jnp.exp(low) + 1.0) * jnp.tanh(0.5 * low))
    act = act.astype(BF)
    edge_s[...] = act[FR - 16 :]
    ext[pl.ds(8, FR), :] = act.astype(F32)

    pl.semaphore_wait(barrier, len(partners))

    edge = push(edge_s, edge_r, right)
    bk = []
    for dl, dc in ((1, 0), (1, 1), (0, 1)):
        to_l, to_c = lax.rem(l + dl, NL), lax.rem(c + dc, NC)
        bk.append(push(wpad_ref.at[to_c], bkr.at[book], dev(l=to_l, c=to_c)))
    bkr[book] = wpad_ref[c]

    eye = lax.broadcasted_iota(I32, (FR, FR), 0) == lax.broadcasted_iota(I32, (FR, FR), 1)
    before = lax.broadcasted_iota(I32, (FR, FR), 0) < lax.broadcasted_iota(I32, (FR, FR), 1)
    row = owner_ref[...].astype(F32)
    row_b = jnp.broadcast_to(row, (FR, FR))
    col = jnp.sum(jnp.where(eye, row_b, 0.0), axis=1, keepdims=True)
    same = jnp.where(before, jnp.where(jnp.broadcast_to(col, (FR, FR)) == row_b, 1.0, 0.0), 0.0)
    rank = jnp.sum(same, axis=0, keepdims=True).astype(I32)
    own = owner_ref[...]
    own_h, own_z, own_x = own >> 5, (own >> 2) & (NZ - 1), own & (NX - 1)
    slot_row = (((own_x * NZ + own_z) * NH + own_h) * CAP + rank).astype(F32)
    slot_col = jnp.sum(
        jnp.where(eye, jnp.broadcast_to(slot_row, (FR, FR)), 0.0), axis=1, keepdims=True
    )
    place_t = jnp.where(
        lax.broadcasted_iota(I32, (ROWS, FR), 0).astype(F32)
        == jnp.broadcast_to(slot_row, (ROWS, FR)), 1.0, 0.0,
    ).astype(BF)
    place = jnp.where(
        lax.broadcasted_iota(I32, (FR, ROWS), 1).astype(F32)
        == jnp.broadcast_to(slot_col, (FR, ROWS)), 1.0, 0.0,
    ).astype(BF)

    pos = seq * FR + lax.broadcasted_iota(I32, (FR, 1), 0)
    starts = []
    total = jnp.int32(0)
    for i in range(lens_ref.shape[1]):
        starts.append(total)
        total = total + lens_ref[0, i]

    def start_of(p):
        best = jnp.zeros_like(p)
        for s in starts:
            best = jnp.maximum(best, jnp.where(p >= s, s, 0))
        return best

    start_here = start_of(pos)
    masks = [jnp.where(pos - k >= start_here, 1.0, 0.0) for k in range(3)]
    back_masks = [masks[0]]
    for k in (1, 2):
        ok = jnp.where(pos >= start_of(pos + k), 1.0, 0.0)
        back_masks.append(ok * jnp.where(pos + k < NSEQ * FR, 1.0, 0.0))

    landed(bk)
    block = bkr[0].astype(F32)
    for i in range(1, 4):
        block = block + bkr[i].astype(F32)
    wf[c, h, z, x] = block.astype(BF)
    mine = wf.at[c, h, z, x]
    w_h = spread(NH, h, lambda p: mine, mine, dev_h)

    load_w.wait()
    edge.wait_recv()
    ext[pl.ds(0, 8), :] = edge_r[...].astype(F32)[8:]
    latent = None
    for k in range(3):
        w = (ext[pl.ds(8 - k, FR), :] * masks[k]).astype(BF)
        win[k] = w
        term = dot(w, wenc[k], NN)
        latent = term if latent is None else latent + term
    latent = latent.astype(BF)
    outgoing = dot(place_t, latent, NN)
    for i in range(NX * NZ):
        a_out[i // NZ, i % NZ] = outgoing[8 * i : 8 * i + 8].astype(BF)
    a_x = spread(NX, x, lambda p: a_out.at[p], r1.at[x], dev_x)
    r1[x] = a_out[x]

    landed(w_h)
    slab = wf.at[c, :, z, x]
    w_z = spread(NZ, z, lambda p: slab, slab, dev_z)

    landed(a_x)
    a_z = spread(NZ, z, lambda p: r1.at[:, p], r2.at[z], dev_z)
    r2[z] = r1[:, z]

    landed(w_z)
    slab = wf.at[c, :, :, x]
    w_x = spread(NX, x, lambda p: slab, slab, dev_x)
    w_c = [push(slab, slab, dev_c(other))]

    jj = lax.broadcasted_iota(I32, (ROWS, ROWS), 0)
    ii = lax.broadcasted_iota(I32, (ROWS, ROWS), 1)
    landed(a_z)
    rows_in = jnp.concatenate(
        [r2[i // NX, i % NX].astype(F32) for i in range(NX * NZ)], axis=0
    ).astype(BF)
    sent_from = ((jj >> 1) & 31) * 8 + (jj >> 6) * 2 + (jj & 1)
    perm = jnp.where(ii == sent_from, 1.0, 0.0).astype(BF)
    moved = dot(perm, rows_in, NN).astype(BF)
    for i in range(NH):
        pbuf[i] = moved[64 * i : 64 * i + 64]
    a_h = spread(NH, h, lambda p: pbuf.at[p], r3.at[h], dev_h)
    r3[h] = pbuf[h]

    order = sorted(range(1, NX), key=lambda d: -min(d, NX - d))
    for copy, d in sorted(zip(w_x, order), key=lambda cd: min(cd[1], NX - cd[1])):
        copy.wait_recv()
        part = wf.at[c, :, :, lax.rem(x + NX - d, NX)]
        w_c.append(push(part, part, dev_c(other)))

    landed(a_h)
    for i in range(NH):
        block = r3[i]
        arr2[0, pl.ds(64 * i, 64), :] = block[:, :128]
        arr2[1, pl.ds(64 * i, 64), :] = block[:, 128:]
    landed(w_c)
    load_c.wait()

    arrived = jnp.concatenate([arr2[0], arr2[1]], axis=1)
    for i in range(NH):
        w0 = wf[0, i].reshape(DM // NH, 128)
        w1 = wf[1, i].reshape(DM // NH, 128)
        wide = jnp.concatenate([w0, w1], axis=1)
        hid[:, i * (DM // NH) : (i + 1) * (DM // NH)] = dot(arrived, wide, NT)
    gain = gain_ref[...]
    gacc[...] = jnp.zeros_like(gacc)

    def norm_rows(i, carry):
        at = pl.ds(pl.multiple_of(i * 16, 16), 16)
        hidden = hid[at, :]
        grad = cot[at, :].astype(F32)
        inv = lax.rsqrt(jnp.mean(hidden * hidden, axis=1, keepdims=True) + EPS)
        normed = hidden * inv
        scaled = grad * gain
        mean = jnp.mean(scaled * normed, axis=1, keepdims=True)
        hg[at, :] = (inv * (scaled - normed * mean)).astype(BF)
        prod = grad * normed
        gacc[...] += prod[:8] + prod[8:]
        return carry

    lax.fori_loop(0, ROWS // 16, norm_rows, 0)

    back = None
    for i in range(NH):
        w0 = wf[0, i].reshape(DM // NH, 128)
        w1 = wf[1, i].reshape(DM // NH, 128)
        wide = jnp.concatenate([w0, w1], axis=1)
        term = dot(hg[:, i * (DM // NH) : (i + 1) * (DM // NH)], wide, NN)
        back = term if back is None else back + term
    back = back.astype(BF)
    for i in range(NH):
        lbuf[i] = back[64 * i : 64 * i + 64]
    l_h = spread(NH, h, lambda p: lbuf.at[p], b1.at[h], dev_h)
    b1[h] = lbuf[h]

    gs[0] = jnp.sum(gacc[...], axis=0, keepdims=True)
    g_c = [push(gs.at[0], gcr.at[c], dev_c(other))]
    gcr[c] = gs[0]
    for i in range(NH):
        at = slice(i * (DM // NH), (i + 1) * (DM // NH))
        as0[at, :] = dot(hg[:, at], arr2[other], TN).astype(BF)
    p_c = [push(as0, ar0, dev_c(other))]
    for i in range(NH):
        at = slice(i * (DM // NH), (i + 1) * (DM // NH))
        aown[at, :] = dot(hg[:, at], arr2[c], TN)

    landed(l_h)
    rows_in = jnp.concatenate([b1[i] for i in range(NH)], axis=0)
    sent_from = ((jj >> 1) & 3) * 64 + (jj >> 3) * 2 + (jj & 1)
    perm = jnp.where(ii == sent_from, 1.0, 0.0).astype(BF)
    moved = dot(perm, rows_in, NN)
    for i in range(NX * NZ):
        c2[i // NX, i % NX] = moved[8 * i : 8 * i + 8].astype(BF)
    l_z = spread(NZ, z, lambda p: c2.at[p], b2.at[z], dev_z)
    b2[z] = c2[z]

    landed(p_c)
    for i in range(NH):
        at = slice(i * (DM // NH), (i + 1) * (DM // NH))
        both = aown[at, :] + ar0[at, :].astype(F32)
        s0[i] = both.astype(BF).reshape(NZ, NX, 16, 128)
    p_x = spread(NX, x, lambda p: s0.at[:, :, p], axr.at[x], dev_x)
    axr[x] = s0[:, :, x]
    landed(g_c)
    gs[1] = gcr[0] + gcr[1]
    g_x = spread(NX, x, lambda p: gs.at[1], gxr.at[x], dev_x)
    gxr[x] = gs[1]

    landed(l_z)
    l_x = spread(NX, x, lambda p: b2.at[:, p], b3.at[x], dev_x)
    b3[x] = b2[:, x]

    landed(l_x)
    returned = jnp.concatenate(
        [b3[i // NZ, i % NZ].astype(F32) for i in range(NX * NZ)], axis=0
    ).astype(BF)
    lat_grad_wide = dot(place, returned, NN)
    lat_grad = lat_grad_wide.astype(BF)
    edge2_s[...] = lat_grad[:16]
    edge2 = push(edge2_s, edge2_r, left)
    for k in range(3):
        part = dot(win[k], lat_grad, TN)
        efull[k] = part
        for i in range(NL):
            for j in range(NC):
                at = (i * NC + j) * 128
                es0[j, k, i] = part[at : at + 128].astype(BF)
    e_c = [push(es0.at[other], er0, dev_c(other))]
    lext[pl.ds(0, FR), :] = lat_grad.astype(F32)

    landed(p_x)
    for i in range(NH):
        acc = axr[0, i].astype(F32)
        for j in range(1, NX):
            acc = acc + axr[j, i].astype(F32)
        s1[i] = acc.astype(BF)
    p_z = spread(NZ, z, lambda p: s1.at[:, p], azr.at[z], dev_z)
    azr[z] = s1[:, z]
    landed(g_x)
    acc = gxr[0]
    for j in range(1, NX):
        acc = acc + gxr[j]
    gs[2] = acc
    g_z = spread(NZ, z, lambda p: gs.at[2], gzr.at[z], dev_z)
    gzr[z] = gs[2]

    landed(e_c)
    for k in range(3):
        for i in range(NL):
            at = pl.ds(pl.multiple_of((i * NC + c) * 128, 128), 128)
            both = efull[k, at, :] + er0[k, i].astype(F32)
            both = both.astype(BF)
            for j in range(NX):
                exs[j, k, i] = both[32 * j : 32 * j + 32]
    e_x = spread(NX, x, lambda p: exs.at[p], exr.at[x], dev_x)
    exr[x] = exs[x]

    landed(p_z)
    for i in range(NH):
        acc = azr[0, i].astype(F32)
        for j in range(1, NZ):
            acc = acc + azr[j, i].astype(F32)
        s2[NL * i] = acc[:8]
        s2[NL * i + 1] = acc[8:]
    p_y = spread(NY, y, lambda p: s2.at[p], ayr.at[y], dev_y)
    ayr[y] = s2[y]
    landed(g_z)
    acc = gzr[0]
    for j in range(1, NZ):
        acc = acc + gzr[j]
    gs[3] = acc
    g_y = spread(NY, y, lambda p: gs.at[3], gyr.at[y], dev_y)
    gyr[y] = gs[3]

    edge2.wait_recv()
    lext[pl.ds(FR, 8), :] = edge2_r[...].astype(F32)[:8]
    act_grad = None
    for k in range(3):
        w = (lext[pl.ds(k, FR), :] * back_masks[k]).astype(BF)
        term = dot(w, wenc[k], NT)
        act_grad = term if act_grad is None else act_grad + term
    feats = feat_ref[...].astype(F32)
    slope = jnp.where(feats > 0, 1.0, jnp.exp(feats))
    gf_ref[...] = (slope * act_grad).astype(BF)

    landed(e_x)
    for i in range(NL):
        for k in range(3):
            acc = exr[0, k, i].astype(F32)
            for j in range(1, NX):
                acc = acc + exr[j, k, i].astype(F32)
            for j in range(NZ):
                r, q = j // 2, j % 2
                ezs[j, i, k] = acc[8 * r : 8 * r + 8, 128 * q : 128 * q + 128].astype(BF)
    e_z = spread(NZ, z, lambda p: ezs.at[p], ezr.at[z], dev_z)
    ezr[z] = ezs[z]

    landed(p_y)
    acc = ayr[0]
    for j in range(1, NY):
        acc = acc + ayr[j]
    s3[...] = acc
    p_f = [push(s3, acr.at[c], dev_c(other))]
    acr[c] = s3[...]
    landed(g_y)
    acc = gyr[0]
    for j in range(1, NY):
        acc = acc + gyr[j]
    gg_ref[...] = acc

    landed(e_z)
    for i in range(NL):
        for k in range(3):
            acc = ezr[0, i, k].astype(F32)
            for j in range(1, NZ):
                acc = acc + ezr[j, i, k].astype(F32)
            eys[i, k] = acc.astype(BF)
    e_y = spread(NY, y, lambda p: eys.at[p % NL], eyr.at[y], dev_y)
    eyr[y] = eys[l]

    landed(p_f)
    low, high = acr[0], acr[1]
    both = jnp.concatenate([low, high], axis=1)
    gw_ref[...] = jnp.where(c == 0, both[:4], both[4:])

    landed(e_y)
    for k in range(3):
        acc = eyr[0, k].astype(F32)
        for j in range(1, NY):
            acc = acc + eyr[j, k].astype(F32)
        gz[z, k] = acc.astype(BF)
    mine_z = gz.at[z]
    o_z = spread(NZ, z, lambda p: mine_z, mine_z, dev_z)
    landed(o_z)
    o_x = spread(NX, x, lambda p: gz, gx.at[x], dev_x)
    gx[x] = gz[...]
    landed(o_x)
    for i in range(NX):
        for j in range(NZ):
            r, q = j // 2, j % 2
            for k in range(3):
                ge_ref[k, 32 * i + 8 * r : 32 * i + 8 * r + 8, 128 * q : 128 * q + 128] = gx[
                    i, j, k
                ].astype(F32)

    for copy in started:
        copy.wait_send()
    assert count[0] <= NSEM


def per_device(features, lengths, owner, w_enc, w_in, gain, cotangent):
    book = lax.axis_index("book")
    tall = jnp.tile(w_in.T, (4, 1))
    here = (jnp.arange(16, dtype=I32) // 4 == book)[:, None]
    padded = jnp.where(here, tall, jnp.zeros_like(tall))
    padded = padded.reshape(16, 2, 128).transpose(1, 0, 2)

    vmem = pl.BlockSpec(memory_space=pltpu.VMEM)
    anyspace = pl.BlockSpec(memory_space=pl.ANY)
    V = pltpu.VMEM
    scratch = [
        V((ROWS, DM), BF), V((3, CH, LAT), BF), V((8 + FR, CH), F32),
        V((16, CH), BF), V((16, CH), BF), V((3, FR, CH), BF),
        V((4, 16, 128), BF), V((2, NH, NZ, NX, 16, 128), BF),
        V((NX, NZ, 8, LAT), BF), V((NX, NZ, 8, LAT), BF), V((NZ, NX, 8, LAT), BF),
        V((NH, 64, LAT), BF), V((NH, 64, LAT), BF), V((2, ROWS, 128), BF),
        V((ROWS, DM), F32), V((ROWS, DM), BF),
        V((NH, 64, LAT), BF), V((NH, 64, LAT), BF), V((NZ, NX, 8, LAT), BF),
        V((NZ, NX, 8, LAT), BF), V((NX, NZ, 8, LAT), BF), V((FR + 8, LAT), F32),
        V((16, LAT), BF), V((16, LAT), BF),
        V((DM, 128), BF), V((DM, 128), BF), V((DM, 128), F32),
        V((NH, NZ, NX, 16, 128), BF), V((NX, NH, NZ, 16, 128), BF),
        V((NH, NZ, 16, 128), BF), V((NZ, NH, 16, 128), BF),
        V((NY, 8, 128), F32), V((NY, 8, 128), F32), V((8, 128), F32), V((2, 8, 128), F32),
        V((4, 1, DM), F32), V((NC, 1, DM), F32), V((NX, 1, DM), F32),
        V((NZ, 1, DM), F32), V((NY, 1, DM), F32), V((8, DM), F32),
        V((3, CH, LAT), F32), V((NC, 3, NL, 128, LAT), BF), V((3, NL, 128, LAT), BF),
        V((NX, 3, NL, 32, LAT), BF), V((NX, 3, NL, 32, LAT), BF),
        V((NZ, NL, 3, 8, 128), BF), V((NZ, NL, 3, 8, 128), BF),
        V((NL, 3, 8, 128), BF), V((NY, 3, 8, 128), BF),
        V((NZ, 3, 8, 128), BF), V((NX, NZ, 3, 8, 128), BF),
        pltpu.SemaphoreType.DMA((NSEM,)), pltpu.SemaphoreType.DMA((NSEM,)),
        pltpu.SemaphoreType.DMA((2,)),
    ]
    gf, ge, gw, gg = pl.pallas_call(
        kernel,
        out_shape=(
            jax.ShapeDtypeStruct((FR, CH), BF),
            jax.ShapeDtypeStruct((3, CH // 4, LAT), F32),
            jax.ShapeDtypeStruct((4, LAT), F32),
            jax.ShapeDtypeStruct((1, DM), F32),
        ),
        in_specs=[vmem, pl.BlockSpec(memory_space=pltpu.SMEM), vmem, vmem, vmem, anyspace, anyspace],
        out_specs=(vmem, vmem, vmem, vmem),
        scratch_shapes=scratch,
        compiler_params=pltpu.CompilerParams(
            collective_id=0, has_side_effects=True, vmem_limit_bytes=48 << 20
        ),
        name="encoder_back",
    )(
        features[0], lengths, owner.reshape(1, FR), padded, gain.reshape(1, DM),
        w_enc, cotangent[0],
    )
    return gf[None], ge, gw.T, gg.reshape(DM)


def solution(mesh):
    placed = (
        P("book", "seq", None),
        P("book", None),
        P("book", "seq", None),
        P(),
        P(None, ("seq", "book")),
        P(),
        P("book", "seq", None),
    )
    return jax.shard_map(
        per_device,
        mesh=mesh,
        in_specs=placed,
        out_specs=(P("book", "seq", None), P(None, "book", None), P(None, ("seq", "book")), P()),
        check_vma=False,
    )
```

time: 1100 us -> 93.5 us (0.09)
  the two profiles are of different devices: /device:TPU:1 before, /device:TPU:8 now
where the time goes in v1:
time: 93.5 us; the launch traced here: 93.2 us
  Pallas kernels  85.3 us (91%)
  local copies, waits for them, and re-layouts  7.16 us (8%)
    pallas_call x1, Pallas kernels, per_device(): pl.pallas_call(kernel, out_shape=(jax.ShapeDtypeStruct((FR, CH), BF), jax...  85.3 us
    unnamed x18, local copies, waits for them, and re-layouts  7.14 us

profile of v1, /device:TPU:8, one launch (start us, length us, event | category | flops | bytes accessed | tf_op | source)
XLA Modules:
  0.0 93.2 jit_solution(8794099351965081785)
XLA Ops:
  0.6 0.0 copy-start.6
  0.7 0.7 copy-done.6
  1.4 0.0 copy-start.3
  1.4 0.0 copy-start.4
  1.4 0.0 copy-start.5
  1.4 0.1 fusion.wpad_ref
  1.5 0.6 copy-done.3
  2.1 0.0 copy-done.4
  2.1 0.0 copy-done.5
  2.1 0.0 copy-start
  2.1 1.2 %copy-done = bf16[1,256,2048]{2,1,0:T(8,128)(2,1)S(1)} copy-done((bf16[1,256,2048]{2,1,0:T(8,128)(2,1)S(1)}, bf16[1,256,2048]{2,1,0:T(8,128)(2,1)}, u32[]{:S(2)}) %copy-start) | copy-done | bytes 1048600
  3.3 0.0 copy-start.1
  3.3 1.1 %copy-done.1 = bf16[3,512,256]{2,1,0:T(8,128)(2,1)S(1)} copy-done((bf16[3,512,256]{2,1,0:T(8,128)(2,1)S(1)}, bf16[3,512,256]{2,1,0:T(8,128)(2,1)}, u32[]{:S(2)}) %copy-start.1) | copy-done | bytes 786456
  4.4 0.0 copy-start.2
  4.4 0.9 copy-done.2
  5.3 85.3 %encoder_back.1 = (bf16[128,512]{1,0:T(8,128)(2,1)S(1)}, f32[3,128,256]{2,1,0:T(8,128)S(1)}, f32[4,256]{1,0:T(4,128)S(1)}, f32[1,2048]{1,0:T(1,128)S(1)}) custom-call(bf16[128,512]{1,0:T(8,128)(2,1)S(1)} %bitcast.11, s32[1,8]{1,0:T(1,128)S(1)} %copy-done.4, s32[1,128]{1,0:T(1,128)S(1)} %bitcast.16, bf16[2,16,128]{2,1,0:T(8,128)(2,1)S(1)} %fusion.wpad_ref, ...), custom_call_target="tpu_custom_call" | custom-call | tf_op jit(solution)/shard_map/encoder_back/pallas_call | solution.py:478
  90.6 0.7 copy.19
  91.3 0.7 copy.20
  92.0 0.6 copy.21
  92.6 0.6 copy.22
  (3 shorter events, 0.0 us)
Async XLA Ops:
  0.6 0.7 copy-start.6
  1.4 0.7 copy-start.3
  1.4 0.7 copy-start.4
  1.4 0.7 copy-start.5
  2.1 1.2 %copy-start = (bf16[1,256,2048]{2,1,0:T(8,128)(2,1)S(1)}, bf16[1,256,2048]{2,1,0:T(8,128)(2,1)}, u32[]{:S(2)}) copy-start(bf16[1,256,2048]{2,1,0:T(8,128)(2,1)} %param.13) | copy-start | bytes 3145732
  3.3 1.1 %copy-start.1 = (bf16[3,512,256]{2,1,0:T(8,128)(2,1)S(1)}, bf16[3,512,256]{2,1,0:T(8,128)(2,1)}, u32[]{:S(2)}) copy-start(bf16[3,512,256]{2,1,0:T(8,128)(2,1)} %wenc_any.1) | copy-start | bytes 2359300
  4.4 0.9 copy-start.2
